TPU v7x, 32 devices: a whole 2x2x4 slice. The times are simulated.
32 devices in a mesh: replica: 2 (over y), fsdp: 8 (over z, core), seq: 2 (over x).
Axes of the slice: x: 2, y: 2, z: 4, core: 2. Of those that a mesh axis runs over, the one named last changes fastest.
Arguments:
- series_in: bfloat16 [16, 512, 1280], P(('replica', 'fsdp'), 'seq'), may hold values from -6 to 6
- cotangent: bfloat16 [16, 512, 1280], P(('replica', 'fsdp'), 'seq'), may hold values from -6 to 6
- qkv_weight: bfloat16 [2, 1280, 3840], P(None, 'fsdp'), may hold values from -0.15625 to 0.15625
- out_weight: bfloat16 [2, 1280, 1280], P(None, 'fsdp'), may hold values from -0.625 to 0.625
- up_weight: bfloat16 [2, 1280, 1280], P(None, 'fsdp'), may hold values from -0.15625 to 0.15625
- down_weight: bfloat16 [2, 1280, 1280], P(None, 'fsdp'), may hold values from -0.15625 to 0.15625
- norm_gains: bfloat16 [2, 2, 1280], P(None, None, 'fsdp'), may hold values from 0.25 to 1.75
- up_bias: bfloat16 [2, 1280], P(None, 'fsdp'), may hold values from -3 to 3
- down_bias: bfloat16 [2, 1280], P(None, 'fsdp'), may hold values from -2 to 2
- query_scale: bfloat16 [2, 80], P(None, 'fsdp'), may hold values from -1 to 1
- pad_length: int32 [16], P(('replica', 'fsdp')), may hold values from 0 to 128, as said below
- span_starts: int32 [16, 4], P(('replica', 'fsdp')), may hold values from 0 to 480, as said below
- span_count: int32 [16], P(('replica', 'fsdp')), may hold values from 1 to 4, as said below
Outputs:
- series_out: bfloat16 [16, 512, 1280], P(('replica', 'fsdp'), 'seq')
- input_grad: bfloat16 [16, 512, 1280], P(('replica', 'fsdp'), 'seq')
- grad_qkv: float32 [2, 1280, 3840], P(None, 'fsdp')
- grad_out: float32 [2, 1280, 1280], P(None, 'fsdp')
- grad_up: float32 [2, 1280, 1280], P(None, 'fsdp')
- grad_down: float32 [2, 1280, 1280], P(None, 'fsdp')
- grad_gains: float32 [2, 2, 1280], P(None, None, 'fsdp')
- grad_up_bias: float32 [2, 1280], P(None, 'fsdp')
- grad_down_bias: float32 [2, 1280], P(None, 'fsdp')
- grad_query_scale: float32 [2, 80], P(None, 'fsdp')
Inputs may be any that keep to these rules, and one draw needn't show every extreme that they name: `pad_length`: one series in every draw has exactly 128 padded positions. `span_starts`: slot 0 of every series starts within 31 positions before 256, so it holds positions 255 and 256; spans may intersect. Slot k of series b is used when k < span_count[b].
All inputs are finite; a program needn't handle non-finite values.
Results may differ from a plain program's by a relative error of at most 0.025.
Values may be sent and summed in bfloat16 or wider, within the bound.
A program may use at most 256 MiB of HBM per device.

v0:
```python
import functools
import math

import jax
import jax.numpy as jnp
from jax import lax
from jax.experimental import pallas as pl
from jax.experimental.pallas import tpu as pltpu
from jax.sharding import PartitionSpec as P

HEADS = 16
HEAD = 80
SPAN = 32


EPSILON = 1e-06
SOFT_ONE = 1.442695041
NEG_FILL = -1e30


def visible(pad_length, span_starts, span_count, offset, local_length, total_length):
    query_pos = offset + jnp.arange(local_length, dtype=jnp.int32)
    key_pos = jnp.arange(total_length, dtype=jnp.int32)
    shared = jnp.zeros((span_starts.shape[0], local_length, total_length), dtype=bool)
    for slot_index in range(span_starts.shape[1]):
        slot_start = span_starts[:, slot_index]
        slot_used = slot_index < span_count
        query_in = (
            slot_used[:, None]
            & (query_pos[None, :] >= slot_start[:, None])
            & (query_pos[None, :] < slot_start[:, None] + SPAN)
        )
        key_in = (key_pos[None, :] >= slot_start[:, None]) & (
            key_pos[None, :] < slot_start[:, None] + SPAN
        )
        shared = shared | query_in[:, :, None] & key_in[:, None, :]
    causal = key_pos[None, :] <= query_pos[:, None]
    allowed = (key_pos[None, None, :] >= pad_length[:, None, None]) & (causal[None] | shared)
    return allowed | (key_pos[None, None, :] == query_pos[None, :, None])


def norm_rows(values, scale_gain):
    inverse = lax.rsqrt(jnp.mean(values * values, axis=-1, keepdims=True) + EPSILON)
    return (values * inverse * scale_gain, inverse)


def norm_back(values, inverse, scale_gain, upstream):
    scaled = upstream * scale_gain
    inner_term = jnp.mean(values * scaled, axis=-1, keepdims=True)
    result = inverse * scaled - values * (inverse * inverse * inverse) * inner_term
    return (result, jnp.sum(upstream * values * inverse, axis=0))


def query_factor(query_scale):
    return jax.nn.softplus(query_scale.astype(jnp.float32)) * (SOFT_ONE / math.sqrt(HEAD))


MESH = pl.DeviceIdType.MESH
UNITS = 6
LAG = 1


class Place:
    def __init__(self, nz):
        self.nz = nz
        self.r = lax.axis_index("replica")
        f = lax.axis_index("fsdp")
        self.s = lax.axis_index("seq")
        self.z = lax.div(f, 2)
        self.c = lax.rem(f, 2)
        self.f = f

    def x(self):
        return (self.r, self.f, 1 - self.s)

    def y(self):
        return (1 - self.r, self.f, self.s)

    def core(self):
        return (self.r, self.f + 1 - 2 * self.c, self.s)

    def to(self, d):
        return (self.r, lax.rem(self.z + d, self.nz) * 2 + self.c, self.s)

    def source(self, d):
        return lax.rem(self.z - d + self.nz, self.nz)

    def greet(self):
        barrier = pltpu.get_barrier_semaphore()
        peers = [self.x(), self.y(), self.core()] + [self.to(d) for d in range(1, self.nz)]
        for peer in peers:
            pl.semaphore_signal(barrier, inc=1, device_id=peer, device_id_type=MESH)
        pl.semaphore_wait(barrier, len(peers))


def remote(src, dst, send, recv, device):
    return pltpu.make_async_remote_copy(
        src_ref=src, dst_ref=dst, send_sem=send, recv_sem=recv, device_id=device, device_id_type=MESH
    )


class Gather:
    def __init__(
        self, nz, layers, qkv_ref, out_ref, up_ref, down_ref, small_ref, full_ref, tiny_ref,
        mine, local_sem, keep_sem, zds, zdr, zs, zr, xs, xr, ys, yr, fxs, fxr, fys, fyr, cs, cr, ts, tr,
    ):
        self.__dict__.update(locals())
        self.at = Place(nz)
        self.shard, self.width = out_ref.shape[1], out_ref.shape[2]
        self.half, self.wide = self.shard // 2, self.width // 2
        self.units = layers * UNITS
        self.hops = nz - 1
        self.iterations = self.units + LAG * (self.hops + 2)

    def source(self, way, k):
        return self.at.z - way * k

    def comes(self, way, k):
        z = self.at.z
        return z >= k if way > 0 else z + k < self.nz

    def goes(self, way):
        z = self.at.z
        return z + 1 < self.nz if way > 0 else z >= 1

    def next(self, way):
        at = self.at
        return (at.r, 2 * (at.z + way) + at.c, at.s)

    def slot(self, way, k):
        return 2 * (k - 1) + (0 if way > 0 else 1)

    def block(self, u, z, c, r, s):
        row = pl.multiple_of((2 * z + c) * self.shard + r * self.half, 8)
        col = pl.multiple_of(s * self.wide, 128)
        return self.full_ref.at[u, pl.ds(row, self.half), pl.ds(col, self.wide)]

    def quarter(self, u, z, c, r, s, part):
        step = self.half // 2
        row = pl.multiple_of((2 * z + c) * self.shard + r * self.half + part * step, 8)
        col = pl.multiple_of(s * self.wide, 128)
        return self.full_ref.at[u, pl.ds(row, step), pl.ds(col, self.wide)]

    def own(self, u, c):
        row = pl.multiple_of((2 * self.at.z + c) * self.shard, 8)
        return self.full_ref.at[u, pl.ds(row, self.shard), :]

    def local(self, layer, k):
        if k < 3:
            piece = self.qkv_ref.at[layer, :, pl.ds(k * self.width, self.width)]
        else:
            piece = (self.out_ref, self.up_ref, self.down_ref)[k - 3].at[layer]
        u = layer * UNITS + k
        return pltpu.make_async_copy(piece, self.mine.at[u], self.local_sem.at[u])

    def keep(self, u):
        return pltpu.make_async_copy(self.mine.at[u], self.own(u, self.at.c), self.keep_sem.at[u])

    def z_copy(self, u, way, k):
        at, n = self.at, self.slot(way, k)
        piece = self.block(u, self.source(way, k - 1), at.c, at.r, at.s)
        held = piece
        if k == 1:
            row = pl.multiple_of(at.r * self.half, 16)
            held = self.mine.at[u, pl.ds(row, self.half), pl.ds(pl.multiple_of(at.s * self.wide, 128), self.wide)]
        return remote(held, piece, self.zs.at[u, n], self.zr.at[u, n], self.next(way))

    def z_diag(self, u, way):
        at, n = self.at, 0 if way > 0 else 1
        piece = self.block(u, at.z, at.c, 1 - at.r, 1 - at.s)
        row = pl.multiple_of((1 - at.r) * self.half, 16)
        col = pl.multiple_of((1 - at.s) * self.wide, 128)
        held = self.mine.at[u, pl.ds(row, self.half), pl.ds(col, self.wide)]
        return remote(held, piece, self.zds.at[u, n], self.zdr.at[u, n], self.next(way))

    def z_came(self, u, way, k):
        at, n = self.at, self.slot(way, k)
        piece = self.block(u, self.source(way, k), at.c, at.r, at.s)
        return remote(piece, piece, self.zs.at[u, n], self.zr.at[u, n], self.next(way))

    def x_copy(self, u, way, k):
        at, n = self.at, self.slot(way, k)
        piece = self.block(u, self.source(way, k), at.c, at.r, at.s)
        return remote(piece, piece, self.xs.at[u, n], self.xr.at[u, n], at.x())

    def y_copy(self, u, way, k):
        at, n = self.at, self.slot(way, k)
        piece = self.block(u, self.source(way, k), at.c, at.r, at.s)
        return remote(piece, piece, self.ys.at[u, n], self.yr.at[u, n], at.y())

    def fx_copy(self, u, way, k):
        at, n = self.at, self.slot(way, k)
        piece = self.quarter(u, self.source(way, k), at.c, 1 - at.r, at.s, 1)
        return remote(piece, piece, self.fxs.at[u, n], self.fxr.at[u, n], at.x())

    def fy_copy(self, u, way, k):
        at, n = self.at, self.slot(way, k)
        piece = self.quarter(u, self.source(way, k), at.c, at.r, 1 - at.s, 0)
        return remote(piece, piece, self.fys.at[u, n], self.fyr.at[u, n], at.y())

    def core_own(self, u):
        own, n = self.own(u, self.at.c), 8 * self.hops
        return remote(self.mine.at[u], own, self.cs.at[u, n], self.cr.at[u, n], self.at.core())

    def core_copy(self, u, way, k, which):
        at = self.at
        r = at.r if which in (0, 1) else 1 - at.r
        s = at.s if which in (0, 2) else 1 - at.s
        piece = self.block(u, self.source(way, k), at.c, r, s)
        n = 4 * self.slot(way, k) + which
        return remote(piece, piece, self.cs.at[u, n], self.cr.at[u, n], at.core())

    def tiny(self, d):
        piece = self.tiny_ref.at[self.at.f]
        return remote(piece, piece, self.ts.at[d - 1], self.tr.at[d - 1], self.at.to(d))

    def tiny_core(self, d):
        piece, n = self.tiny_ref.at[2 * self.at.source(d) + self.at.c], self.nz - 1 + d
        return remote(piece, piece, self.ts.at[n], self.tr.at[n], self.at.core())

    def begin(self):
        self.tiny_ref[self.at.f] = self.small_ref[...].astype(jnp.bfloat16)
        for layer in range(self.layers):
            for k in range(UNITS):
                self.local(layer, k).start()
        self.at.greet()
        for d in range(1, self.nz):
            self.tiny(d).start()
        self.tiny_core(0).start()

    def tiny_pass(self):
        for d in range(1, self.nz):
            self.tiny(d).wait_recv()
            self.tiny_core(d).start()

    def tiny_ready(self):
        for d in range(self.nz):
            self.tiny_core(d).wait_recv()

    def tiny_done(self):
        for d in range(1, self.nz):
            self.tiny(d).wait_send()
        for d in range(self.nz):
            self.tiny_core(d).wait_send()

    def when(self, cond, work):
        pl.when(cond)(work)

    def first(self, u):
        pltpu.make_async_copy(self.out_ref.at[0], self.mine.at[u], self.local_sem.at[u]).wait()
        self.keep(u).start()
        for way in (1, -1):
            def work(way=way):
                self.z_copy(u, way, 1).start()
                self.z_diag(u, way).start()
            self.when(self.goes(way), work)
        self.core_own(u).start()

    def hop(self, u, k):
        for way in (1, -1):
            def work(way=way):
                self.z_came(u, way, k).wait_recv()
                if k < self.hops:
                    self.when(self.goes(way), lambda: self.z_copy(u, way, k + 1).start())
                self.x_copy(u, way, k).start()
                self.y_copy(u, way, k).start()
                self.core_copy(u, way, k, 0).start()
                if k == 1:
                    self.z_diag(u, way).wait_recv()
                    self.core_copy(u, way, k, 3).start()
            self.when(self.comes(way, k), work)

    def forward(self, u, k):
        for way in (1, -1):
            def work(way=way):
                self.x_copy(u, way, k).wait_recv()
                if k > 1:
                    self.fy_copy(u, way, k).start()
                self.core_copy(u, way, k, 1).start()
                self.y_copy(u, way, k).wait_recv()
                if k > 1:
                    self.fx_copy(u, way, k).start()
                self.core_copy(u, way, k, 2).start()
            self.when(self.comes(way, k), work)

    def diagonal(self, u, k):
        for way in (1, -1):
            def work(way=way):
                self.fx_copy(u, way, k).wait_recv()
                self.fy_copy(u, way, k).wait_recv()
                self.core_copy(u, way, k, 3).start()
            self.when(self.comes(way, k), work)

    def step(self, i):
        def stage(lag, work):
            u = i - lag
            self.when((u >= 0) & (u < self.units), lambda: work(u))

        stage(0, self.first)
        for k in range(1, self.hops + 1):
            stage(LAG * k, lambda u, k=k: self.hop(u, k))
        for k in range(1, self.hops + 1):
            stage(LAG * (k + 1), lambda u, k=k: self.forward(u, k))
        for k in range(2, self.hops + 1):
            stage(LAG * (k + 2), lambda u, k=k: self.diagonal(u, k))

    def ready(self, u):
        self.keep(u).wait()
        self.core_own(u).wait_recv()
        for k in range(1, self.hops + 1):
            for way in (1, -1):
                def work(way=way, k=k):
                    for which in range(4):
                        self.core_copy(u, way, k, which).wait_recv()
                self.when(self.comes(way, k), work)

    def drain(self, u):
        self.core_own(u).wait_send()
        for k in range(1, self.hops + 1):
            for way in (1, -1):
                def sent(way=way, k=k):
                    self.z_copy(u, way, k).wait_send()
                    if k == 1:
                        self.z_diag(u, way).wait_send()
                came = self.goes(way)
                if k > 1:
                    came = came & self.comes(way, k - 1)
                self.when(came, sent)

                def work(way=way, k=k):
                    copies = (self.x_copy, self.y_copy, self.fx_copy, self.fy_copy)
                    for copy in copies if k > 1 else copies[:2]:
                        copy(u, way, k).wait_send()
                    for which in range(4):
                        self.core_copy(u, way, k, which).wait_send()
                self.when(self.comes(way, k), work)

    def finish(self):
        @pl.loop(0, self.units)
        def _(u):
            self.drain(u)

        self.tiny_done()


def gather_scratch(nz, layers, shard, width):
    units, n = layers * UNITS, 2 * (nz - 1)
    dma = pltpu.SemaphoreType.DMA
    return (
        [pltpu.VMEM((units, shard, width), jnp.bfloat16), dma((units,)), dma((units,))]
        + [dma((units, 2))] * 2
        + [dma((units, n))] * 10
        + [dma((units, 1 + 4 * n))] * 2
        + [dma((2 * nz,))] * 2
    )


def dot_nn(a, b):
    return jnp.dot(a, b, preferred_element_type=jnp.float32)


def dot_nt(a, b):
    return lax.dot_general(a, b, (((1,), (1,)), ((), ())), preferred_element_type=jnp.float32)


def dot_tn(a, b):
    return lax.dot_general(a, b, (((0,), (0,)), ((), ())), preferred_element_type=jnp.float32)


ROWS = 128
TALL = 256
BEGIN = 3


def each_tile(count, body, rows=ROWS):
    @pl.loop(0, count // rows)
    def _(i):
        body(pl.ds(pl.multiple_of(i * rows, rows), rows))


def head_rows(h):
    return pl.ds(pl.multiple_of(h * HEAD, 16), HEAD)


def row_norm(values, gain):
    inverse = lax.rsqrt(jnp.mean(values * values, axis=-1, keepdims=True) + EPSILON)
    return (values * inverse * gain).astype(jnp.bfloat16)


def expand_small(tiny_ref, vec_ref, layers, shard, part):
    width = vec_ref.shape[1]
    count = tiny_ref.shape[0]
    rows, lanes = tiny_ref.shape[1:]
    line = lax.broadcasted_iota(jnp.int32, (lanes, width), 0)
    column = lax.broadcasted_iota(jnp.int32, (lanes, width), 1)
    inner = lax.rem(column, HEAD)

    def place(f, sums):
        plain, scale = sums
        piece = tiny_ref[f]
        hot = jnp.where((column - f * shard == line) & (line < shard), 1.0, 0.0).astype(jnp.bfloat16)
        spread = jnp.where((inner - f * part == line) & (line < part), 1.0, 0.0).astype(jnp.bfloat16)
        return plain + dot_nn(piece, hot), scale + dot_nn(piece, spread)

    zero = jnp.zeros((rows, width), jnp.float32)
    plain, scale = lax.fori_loop(0, count, place, (zero, zero))
    soft = jnp.maximum(scale, 0.0) + jnp.log(1.0 + jnp.exp(-jnp.abs(scale)))
    row = lax.broadcasted_iota(jnp.int32, (rows, width), 0)
    vec_ref[...] = jnp.where(row < 4 * layers, plain, soft * (SOFT_ONE / math.sqrt(HEAD)))


def attend(heads, q_ref, k_ref, v_ref, bias_ref, out_ref, lse_ref):
    queries = q_ref.shape[1]

    @pl.loop(*heads)
    def _(h):
        rows = head_rows(h)
        scores = dot_tn(k_ref[rows, :], q_ref[rows, :]) + bias_ref[:, :queries]
        top = jnp.max(scores, axis=0, keepdims=True)
        grown = jnp.exp(scores - top)
        total = jnp.sum(grown, axis=0, keepdims=True)
        out = dot_nn(v_ref[rows, :], grown.astype(jnp.bfloat16)) * (1.0 / total)
        out_ref[rows, :] = out.astype(jnp.bfloat16)
        lse_ref[h] = top + jnp.log(total)


def forward_kernel(nz, layers, part, *refs):
    series_ref, qkv_ref, out_ref, up_ref, down_ref = refs[:5]
    gains_ref, up_bias_ref, down_bias_ref, scale_ref, pad_ref, starts_ref, count_ref = refs[5:12]
    full_ref, vec_out, series_out, bias_out = refs[12:16]
    per = 11
    saved = [refs[16 + per * l : 16 + per * (l + 1)] for l in range(layers)]
    refs = refs[16 + per * layers :]
    names = ("current", "normed_t", "q", "k", "v", "lse", "att", "after", "mixed", "pre", "hidden")
    held = [dict(zip(names, refs[per * l : per * (l + 1)])) for l in range(layers)]
    refs = refs[per * layers :]
    normed, weights, vec, last, tiny_ref, small_ref, bias_ref, swap_sem, load_sem, save_sem = refs[:10]
    gather = Gather(
        nz, layers, qkv_ref, out_ref, up_ref, down_ref, small_ref, full_ref, tiny_ref, *refs[10:]
    )
    at = gather.at
    length = series_ref.shape[0]
    total = held[0]["normed_t"].shape[1]
    other = total - length

    own_copy = pltpu.make_async_copy(series_ref, held[0]["current"].at[pl.ds(0, length)], swap_sem.at[0])
    swap_copy = remote(
        series_ref, held[0]["current"].at[pl.ds(length, other)], swap_sem.at[1], swap_sem.at[2], at.x()
    )

    def save(l, n):
        return pltpu.make_async_copy(held[l][names[n]], saved[l][n], save_sem.at[l, n])

    def fetch(u):
        return pltpu.make_async_copy(full_ref.at[u], weights.at[u % 2], load_sem.at[u % 2])

    def arrived(u):
        fetch(u).wait()
        return weights.at[u % 2]

    def vector(n):
        return vec[n : n + 1, :]

    def normalize(l):
        b = held[l]
        gain = vector(2 * l)

        def body(r):
            values = row_norm(b["current"][r, :].astype(jnp.float32), gain)
            normed[r, :] = values
            b["normed_t"][:, r] = values.T
        each_tile(total, body)
        save(l, 1).start()

    def project(l, n):
        b = held[l]
        target = b[("q", "k", "v")[n]]
        weight = arrived(l * UNITS + n)

        def body(r):
            values = dot_nn(normed[r, :], weight[...])
            if n == 0:
                values = values * vector(4 * layers + l)
            target[:, r] = values.astype(jnp.bfloat16).T
        each_tile(target.shape[1], body)
        save(l, 2 + n).start()

    def attention(l, first):
        b = held[l]
        heads = (0, HEADS // 2) if first else (HEADS // 2, HEADS)
        attend(heads, b["q"], b["k"], b["v"], bias_ref, b["att"], b["lse"])
        if not first:
            save(l, 5).start()
            save(l, 6).start()

    def output(l):
        b = held[l]
        weight = arrived(l * UNITS + 3)
        gain = vector(2 * l + 1)

        def body(r):
            after = b["current"][r, :].astype(jnp.float32) + dot_tn(b["att"][:, r], weight[...])
            b["after"][r, :] = after
            b["mixed"][r, :] = row_norm(after, gain)
        each_tile(b["after"].shape[0], body)
        save(l, 7).start()
        save(l, 8).start()

    def expand(l):
        b = held[l]
        weight = arrived(l * UNITS + 4)
        bias = vector(2 * layers + l)

        def body(r):
            pre = dot_nn(b["mixed"][r, :], weight[...]) + bias
            b["pre"][r, :] = pre
            b["hidden"][r, :] = (pre * (1.0 / (1.0 + jnp.exp(-pre)))).astype(jnp.bfloat16)
        each_tile(b["pre"].shape[0], body)
        save(l, 9).start()
        save(l, 10).start()

    def contract(l):
        b = held[l]
        weight = arrived(l * UNITS + 5)
        bias = vector(3 * layers + l)

        def body(r):
            values = b["after"][r, :] + (dot_nn(b["hidden"][r, :], weight[...]) + bias)
            if l + 1 < layers:
                held[l + 1]["current"][r, :] = values
            else:
                last[r, :] = values.astype(jnp.bfloat16)
        each_tile(b["after"].shape[0], body)
        if l + 1 < layers:
            save(l + 1, 0).start()
            normalize(l + 1)
        else:
            pltpu.make_async_copy(last, series_out, swap_sem.at[3]).start()

    tasks = {}

    def add(i, work):
        tasks.setdefault(i, []).append(work)

    lag = gather.iterations - layers * UNITS

    def early():
        gather.tiny_pass()
        gather.tiny_ready()
        expand_small(tiny_ref, vec, layers, gather.shard, part)
        pltpu.make_async_copy(vec, vec_out, swap_sem.at[4]).start()
        fill_bias(bias_ref, length, pad_ref, starts_ref, count_ref)
        pltpu.make_async_copy(bias_ref, bias_out, swap_sem.at[5]).start()

    def begin():
        own_copy.wait()
        swap_copy.wait_recv()
        save(0, 0).start()
        normalize(0)

    def pull(u):
        gather.ready(u)
        fetch(u).start()

    add(1, early)
    add(BEGIN, begin)
    units = layers * UNITS
    computing = []
    for l in range(layers):
        computing += [[lambda l=l, n=n: project(l, n)] for n in range(3)]
        computing[-1].append(lambda l=l: attention(l, True))
        computing.append([lambda l=l: attention(l, False), lambda l=l: output(l)])
        computing.append([lambda l=l: expand(l)])
        computing.append([lambda l=l: contract(l)])
    for u in range(units):
        add(u + lag, lambda u=u: pull(u))
        for one in computing[u]:
            add(min(u + lag + 1, gather.iterations - 1), one)

    own_copy.start()
    small_ref[...] = jnp.zeros_like(small_ref)
    shard = gather.shard
    for l in range(layers):
        for n in range(2):
            small_ref[2 * l + n : 2 * l + n + 1, :shard] = gains_ref[l, n : n + 1, :].astype(jnp.float32)
    groups = ((2 * layers, up_bias_ref, shard), (3 * layers, down_bias_ref, shard), (4 * layers, scale_ref, part))
    for base, ref, size in groups:
        small_ref[base : base + layers, :size] = ref[...].astype(jnp.float32)
    gather.begin()
    swap_copy.start()

    @pl.loop(0, gather.iterations)
    def _(i):
        gather.step(i)
        for when, work in sorted(tasks.items()):
            @pl.when(i == when)
            def _(work=work):
                for one in work:
                    one()

    swap_copy.wait_send()
    pltpu.make_async_copy(last, series_out, swap_sem.at[3]).wait()
    pltpu.make_async_copy(vec, vec_out, swap_sem.at[4]).wait()
    pltpu.make_async_copy(bias_ref, bias_out, swap_sem.at[5]).wait()
    for l in range(layers):
        for n in range(per):
            save(l, n).wait()
    gather.finish()


def saved_shapes(layers, length, total, width):
    low, wide = jnp.bfloat16, jnp.float32
    shapes = []
    for l in range(layers):
        count = length if l == layers - 1 else total
        kind = low if l == 0 else wide
        shapes.append(
            [
                ((total, width), kind),
                ((width, total), low),
                ((width, count), low),
                ((width, total), low),
                ((width, total), low),
                ((HEADS, 1, count), wide),
                ((width, count), low),
                ((count, width), wide),
                ((count, width), low),
                ((count, width), wide),
                ((count, width), low),
            ]
        )
    return shapes


def forward_pass(nz, series, matrices, vectors, spans):
    layers, shard, width = matrices[1].shape
    length, part = series.shape[0], vectors[3].shape[1]
    total = 2 * length
    units = layers * UNITS
    low, wide = jnp.bfloat16, jnp.float32
    shapes = [one for group in saved_shapes(layers, length, total, width) for one in group]
    small = (5 * layers + -5 * layers % 16, shard + -shard % 128)
    dma = pltpu.SemaphoreType.DMA
    anywhere = pl.BlockSpec(memory_space=pl.ANY)
    inside = pl.BlockSpec(memory_space=pltpu.VMEM)
    scalars = pl.BlockSpec(memory_space=pltpu.SMEM)
    count = 2 * nz
    results = pl.pallas_call(
        functools.partial(forward_kernel, nz, layers, part),
        out_shape=(
            jax.ShapeDtypeStruct((units, count * shard, width), low),
            jax.ShapeDtypeStruct((small[0], width), wide),
            jax.ShapeDtypeStruct((length, width), low),
            jax.ShapeDtypeStruct((total, total), wide),
        )
        + tuple(jax.ShapeDtypeStruct(*one) for one in shapes),
        in_specs=[anywhere] * 5 + [inside] * 4 + [scalars] * 3,
        out_specs=(anywhere,) * (4 + len(shapes)),
        scratch_shapes=[pltpu.VMEM(*one) for one in shapes]
        + [
            pltpu.VMEM((total, width), low),
            pltpu.VMEM((2, width, width), low),
            pltpu.VMEM((small[0], width), wide),
            pltpu.VMEM((length, width), low),
            pltpu.VMEM((count,) + small, low),
            pltpu.VMEM(small, wide),
            pltpu.VMEM((total, total), wide),
            dma((6,)),
            dma((2,)),
            dma((layers, 11)),
        ]
        + gather_scratch(nz, layers, shard, width),
        compiler_params=pltpu.CompilerParams(
            collective_id=1, has_side_effects=True, vmem_limit_bytes=60 << 20
        ),
    )(series, *matrices, *vectors, *spans)
    full, vec, out, bias = results[:4]
    saved = [results[4 + 11 * l : 15 + 11 * l] for l in range(layers)]
    return full, vec, out, bias, saved


def fill_bias(bias_ref, length, pad_ref, starts_ref, count_ref):
    s = lax.axis_index("seq")
    total = bias_ref.shape[0]
    pad, count = pad_ref[0], count_ref[0]

    def place(index):
        return jnp.where(index < length, s * length + index, -s * length + index)

    query = place(lax.broadcasted_iota(jnp.int32, (ROWS, total), 1))

    @pl.loop(0, total // ROWS)
    def _(i):
        key = place(lax.broadcasted_iota(jnp.int32, (ROWS, total), 0) + i * ROWS)
        seen = key <= query
        for slot in range(starts_ref.shape[1]):
            start = jnp.where(slot < count, starts_ref[0, slot], -2 * SPAN)
            stop = start + SPAN
            seen = seen | (key >= start) & (key < stop) & (query >= start) & (query < stop)
        allowed = (seen & (key >= pad)) | (key == query)
        rows = pl.ds(pl.multiple_of(i * ROWS, ROWS), ROWS)
        bias_ref[rows, :] = jnp.where(allowed, 0.0, NEG_FILL)


SLOTS = 14
LAGS = (1, 3, 6, 8, 10, 12)


class Reduce:
    def __init__(
        self, nz, units, full_ref, tiny, tiny_out, grads, held, bx, by, near, far, swap, tiny_in,
        as_, ar, bs, br, zs, zr, es, er, ls, ps, pr, ts, tr, free,
    ):
        self.__dict__.update(locals())
        self.at = Place(nz)
        self.slots, _, self.half, self.width = held.shape
        self.shard = 2 * self.half
        self.wide, self.low = self.width // 2, nz // 2
        self.steps = range(1, nz)
        self.parts = 2 * units
        self.iterations = self.parts + LAGS[-1]
        self.side = self.column(self.at.z)

    def column(self, z):
        return jnp.where(z < self.low, self.at.s, self.at.r)

    def cols(self, side):
        return pl.ds(pl.multiple_of(side * self.wide, 128), self.wide)

    def slot(self, h):
        return lax.rem(h, self.slots)

    def band(self, h):
        return pl.ds(pl.multiple_of(lax.rem(h, 2) * self.half, 16), self.half)

    def z_peer(self, d):
        at = self.at
        z = lax.rem(at.z + d, self.nz) if 2 * d == self.nz else at.z + 1 - 2 * lax.rem(at.z, 2)
        return z, (at.r, 2 * z + at.c, at.s)

    def pair_peer(self):
        at, first = self.at, self.at.z < self.low
        return (jnp.where(first, 1 - at.r, at.r), at.f, jnp.where(first, at.s, 1 - at.s))

    def last_peer(self):
        at, first = self.at, self.at.z < self.low
        return (jnp.where(first, at.r, 1 - at.r), at.f, jnp.where(first, 1 - at.s, at.s))

    def a_copy(self, h):
        piece = self.grads.at[:, 1 - self.at.c, self.band(h), :]
        return remote(piece, self.held.at[self.slot(h)], self.as_.at[h], self.ar.at[h], self.at.core())

    def bx_copy(self, h):
        piece = self.held.at[self.slot(h), pl.ds(0, self.low), :, self.cols(1 - self.at.s)]
        return remote(piece, self.bx.at[h], self.bs.at[h, 0], self.br.at[h, 0], self.at.x())

    def by_copy(self, h):
        piece = self.held.at[self.slot(h), pl.ds(self.low, self.low), :, self.cols(1 - self.at.r)]
        return remote(piece, self.by.at[h], self.bs.at[h, 1], self.br.at[h, 1], self.at.y())

    def near_copy(self, h, n):
        target = n * 2 + 1 - lax.rem(self.at.z, 2)
        side = (self.at.s, self.at.r)[n]
        piece = self.held.at[self.slot(h), target, :, self.cols(side)]
        return remote(piece, self.near.at[h, n], self.zs.at[h, n], self.zr.at[h, n], self.z_peer(1)[1])

    def far_copy(self, h):
        z, peer = self.z_peer(2)
        piece = self.held.at[self.slot(h), z, :, self.cols(self.column(z))]
        return remote(piece, self.far.at[h], self.zs.at[h, 2], self.zr.at[h, 2], peer)

    def pair_copy(self, h):
        piece = self.held.at[self.slot(h), self.at.z, :, self.cols(self.side)]
        return remote(piece, self.swap.at[h], self.es.at[h], self.er.at[h], self.pair_peer())

    def spot(self, h):
        return self.full_ref.at[lax.div(h, 2), self.band(h), self.cols(self.side)]

    def put_copy(self, h):
        return pltpu.make_async_copy(self.bx.at[h, 0], self.spot(h), self.ls.at[h])

    def last_copy(self, h):
        return remote(self.bx.at[h, 0], self.spot(h), self.ps.at[h], self.pr.at[h], self.last_peer())

    def plus(self, *values):
        return sum(v.astype(jnp.float32) for v in values).astype(jnp.bfloat16)

    def a_start(self, h):
        @pl.when(h >= self.slots)
        def _():
            pl.semaphore_wait(self.free, 1)
        self.a_copy(h).start()

    def a_stage(self, h):
        held, slot, c = self.held, self.slot(h), self.at.c
        self.a_copy(h).wait_recv()

        @pl.loop(0, self.nz)
        def _(z):
            held[slot, z] = self.plus(held[slot, z], self.grads[z, c, self.band(h), :])
        self.bx_copy(h).start()
        self.by_copy(h).start()
        self.a_copy(h).wait_send()

    def b_stage(self, h):
        held, slot, at = self.held, self.slot(h), self.at
        for copy, came, base, side in (
            (self.bx_copy(h), self.bx, 0, at.s),
            (self.by_copy(h), self.by, self.low, at.r),
        ):
            copy.wait()

            @pl.loop(0, self.low)
            def _(z, came=came, base=base, side=side):
                mine = self.cols(side)
                held[slot, base + z, :, mine] = self.plus(held[slot, base + z, :, mine], came[h, z])
        for n in range(2):
            self.near_copy(h, n).start()

    def near_stage(self, h):
        held, slot, at = self.held, self.slot(h), self.at
        for n in range(2):
            self.near_copy(h, n).wait()
            target, mine = 2 * n + lax.rem(at.z, 2), self.cols((at.s, at.r)[n])
            held[slot, target, :, mine] = self.plus(held[slot, target, :, mine], self.near[h, n])
        self.far_copy(h).start()

    def far_stage(self, h):
        held, slot, z, mine = self.held, self.slot(h), self.at.z, self.cols(self.side)
        self.far_copy(h).wait()
        held[slot, z, :, mine] = self.plus(held[slot, z, :, mine], self.far[h])
        self.pair_copy(h).start()

    def pair_stage(self, h):
        held, slot, z, mine = self.held, self.slot(h), self.at.z, self.cols(self.side)
        self.pair_copy(h).wait()
        self.bx[h, 0] = self.plus(held[slot, z, :, mine], self.swap[h])

        @pl.when(h + self.slots < self.parts)
        def _():
            pl.semaphore_signal(self.free, inc=1, device_id=self.at.core(), device_id_type=MESH)
        self.put_copy(h).start()
        self.last_copy(h).start()

    def close(self, h):
        self.put_copy(h).wait()
        self.last_copy(h).wait()

    def step(self, i):
        def stage(lag, work):
            h = i - lag
            pl.when((h >= 0) & (h < self.parts))(lambda: work(h))

        works = (self.a_stage, self.b_stage, self.near_stage, self.far_stage, self.pair_stage, self.close)
        for lag, work in zip(LAGS, works):
            stage(lag, work)

    def launch(self, i):
        @pl.when((lax.rem(i, 2) == 0) & (i < self.parts))
        def _():
            self.a_start(i)
            self.a_start(i + 1)

    def tiny_copy(self, n, peer):
        return remote(self.tiny, self.tiny_in.at[n], self.ts.at[n], self.tr.at[n], peer)

    def tiny_z(self, d):
        return remote(self.tiny, self.tiny_in.at[2 + d], self.ts.at[2 + d], self.tr.at[2 + d], self.at.to(d))

    def tiny_step(self, n):
        peers = (self.at.core(), self.at.x(), self.at.y())
        if 0 < n <= 3:
            copy = self.tiny_copy(n - 1, peers[n - 1])
            copy.wait()
            self.tiny[...] = self.tiny[...] + self.tiny_in[n - 1]
        if n < 3:
            self.tiny_copy(n, peers[n]).start()
        if n == 3:
            for d in self.steps:
                self.tiny_z(d).start()
        if n == 4:
            for d in self.steps:
                self.tiny_z(d).wait()
            self.tiny_out[...] = self.tiny[...] + sum(self.tiny_in[2 + d] for d in self.steps)


def backward_kernel(nz, layers, length, total, *refs):
    cot_ref, full_ref, vec, bias_ref = refs[:4]
    per = 11
    saved = [refs[4 + per * l : 4 + per * (l + 1)] for l in range(layers)]
    refs = refs[4 + per * layers :]
    share_ref, tiny_out, input_ref = refs[:3]
    (
        up, wide_a, wide_b, hidden, mixed, pre_low, low, trio, att, do, lse, weight, came, sent,
        load_sem, weight_sem, x_sem, tiny, grads,
    ) = refs[3:22]
    units = layers * UNITS
    k, v, q = trio.at[0], trio.at[1], trio.at[2]
    reduce = Reduce(nz, units, share_ref, tiny, tiny_out, grads, *refs[22:])
    at = reduce.at
    width = up.shape[1]
    wide, half_z = width // 2, nz // 2
    shard = reduce.shard
    names = ("current", "normed_t", "q", "k", "v", "lse", "att", "after", "mixed", "pre", "hidden")
    homes = dict(
        normed_t=att, q=q, k=k, v=v, lse=lse, att=att, after=wide_b, mixed=mixed, pre=wide_a, hidden=hidden
    )

    def load(l, name):
        n = names.index(name)
        source = saved[l][n]
        home = homes.get(name, hidden if source.dtype == jnp.bfloat16 else wide_b)
        if home.shape != source.shape:
            if len(source.shape) == 3:
                home = home.at[:, :, pl.ds(0, source.shape[2])]
            elif source.shape[0] != home.shape[0]:
                home = home.at[pl.ds(0, source.shape[0]), :]
            else:
                home = home.at[:, pl.ds(0, source.shape[1])]
        return pltpu.make_async_copy(source, home, load_sem.at[l, n])

    def fetch(u):
        return pltpu.make_async_copy(full_ref.at[u], weight, weight_sem.at[0])

    def fill(product):
        @pl.loop(0, 2)
        def _(i):
            @pl.loop(0, 2)
            def _(j):
                r = pl.ds(pl.multiple_of(i * wide, 128), wide)
                c = pl.ds(pl.multiple_of(j * wide, 128), wide)
                value = product(r, c).astype(jnp.bfloat16).reshape(half_z, 2, shard, wide)
                grads[pl.ds(i * half_z, half_z), :, :, c] = value

    def vector(n):
        return vec[n : n + 1, :]

    def gather_row(n, values):
        tiny[n : n + 1, :] = tiny[n : n + 1, :] + jnp.sum(values, axis=0, keepdims=True)

    def norm_tile(values, gain, w, n):
        inverse = lax.rsqrt(jnp.mean(values * values, axis=-1, keepdims=True) + EPSILON)
        scaled = w * gain
        inner = jnp.mean(values * scaled, axis=-1, keepdims=True)
        gather_row(n, w * values * inverse)
        return inverse * scaled - values * (inverse * inverse * inverse) * inner

    def count(l):
        return length if l == layers - 1 else total

    def next_load(l, *which):
        if l > 0:
            for name in which:
                load(l - 1, name).start()

    def down(l):
        m = count(l)
        load(l, "hidden").wait()

        def body(r):
            value = up[r, :].astype(jnp.bfloat16)
            low[r, :] = value
            gather_row(3 * layers + l, value.astype(jnp.float32))
        each_tile(m, body)
        fill(lambda r, c: dot_tn(hidden[:m, r], low[:m, c]))
        if saved[l][0].dtype == jnp.bfloat16:
            load(l, "current").start()
        else:
            next_load(l, "hidden")

    def expand(l):
        fetch(l * UNITS + 5).wait()
        load(l, "pre").wait()

        def body(r):
            grown = dot_nt(low[r, :], weight[...])
            value = wide_a[r, :]
            gate = 1.0 / (1.0 + jnp.exp(-value))
            result = (grown * gate * (1.0 + value * (1.0 - gate))).astype(jnp.bfloat16)
            pre_low[r, :] = result
            gather_row(2 * layers + l, result.astype(jnp.float32))
        each_tile(count(l), body, TALL)
        fetch(l * UNITS + 4).start()

    def fill_up(l):
        m = count(l)
        load(l, "mixed").wait()
        fill(lambda r, c: dot_tn(mixed[:m, r], pre_low[:m, c]))
        next_load(l, "mixed")

    def output(l):
        fetch(l * UNITS + 4).wait()
        load(l, "after").wait()
        gain = vector(2 * l + 1)

        def body(r):
            w = dot_nt(pre_low[r, :], weight[...])
            value = up[r, :] + norm_tile(wide_b[r, :], gain, w, 2 * l + 1)
            up[r, :] = value
            low[r, :] = value.astype(jnp.bfloat16)
        each_tile(count(l), body, TALL)
        fetch(l * UNITS + 3).start()
        if saved[l][0].dtype != jnp.bfloat16:
            load(l, "current").start()

    def fill_out(l):
        m = count(l)
        load(l, "att").wait()
        fill(lambda r, c: dot_nn(att[r, :m], low[:m, c]))
        load(l, "normed_t").start()

    def attention(l, start, stop):
        m = count(l)
        row = 4 * layers + l
        factor = jnp.broadcast_to(vec[row : row + 1, 0:128], (128, 128)).T[0:HEAD, 0:1]

        def head(h, sums):
            rows = head_rows(h)
            kh, vh, qh, oh = k[rows, :], v[rows, :], q[rows, :m], do[rows, :m]
            scores = dot_tn(kh, qh) + bias_ref[:, :m]
            probs = jnp.exp(scores - lse[h, :, :m])
            weighted = probs * dot_tn(vh, oh)
            inner = jnp.sum(weighted, axis=0, keepdims=True)
            score = (weighted - probs * inner).astype(jnp.bfloat16)
            v[rows, :] = dot_nt(oh, probs.astype(jnp.bfloat16)).astype(jnp.bfloat16)
            k[rows, :] = dot_nt(qh, score).astype(jnp.bfloat16)
            query = dot_nn(kh, score)
            q[rows, :m] = (query * factor).astype(jnp.bfloat16)
            return sums + jnp.sum(query * qh.astype(jnp.float32), axis=1, keepdims=True)

        sums = lax.fori_loop(start, stop, head, jnp.zeros((HEAD, 1), jnp.float32))
        flat = jnp.broadcast_to(sums, (HEAD, 128)).T
        tiny[row : row + 1, 0:HEAD] = tiny[row : row + 1, 0:HEAD] + flat[0:1, :]

    def open_heads(l):
        m = count(l)
        fetch(l * UNITS + 3).wait()

        def body(r):
            do[r, :m] = dot_nt(weight[r, :], low[:m, :]).astype(jnp.bfloat16)
        each_tile(width, body, wide)
        fetch(l * UNITS + 1).start()
        for name in ("q", "k", "v", "lse"):
            load(l, name).wait()

    def turn(l):
        next_load(l, "lse")
        load(l, "normed_t").wait()

    def fill_project(n):
        fill(lambda r, c: dot_nt(att[r, :], trio[n, c, :]))

    def project(l, n):
        fetch(l * UNITS + lax.rem(n + 1, 3)).wait()
        count = jnp.where((n == 2) & (l == layers - 1), length, total)

        @pl.loop(0, lax.div(count, TALL))
        def _(i):
            r = pl.ds(pl.multiple_of(i * TALL, TALL), TALL)
            value = dot_nt(trio[n, :, r].T, weight[...])
            wide_a[r, :] = value + jnp.where(n > 0, wide_a[r, :], 0.0)

    def settle(l, n):
        if n < 2:
            fetch(l * UNITS + (2, 0)[n]).start()
            return
        if l > 0:
            fetch((l - 1) * UNITS + 5).start()
        load(l, "current").wait()
        gain = vector(2 * l)
        current = hidden if saved[l][0].dtype == jnp.bfloat16 else wide_b

        def close(r):
            return norm_tile(current[r, :].astype(jnp.float32), gain, wide_a[r, :], 2 * l)

        own = count(l)

        def first(r):
            up[r, :] = up[r, :] + close(r)
        each_tile(own, first)
        if own < total:
            @pl.loop(own // ROWS, total // ROWS)
            def _(i):
                r = pl.ds(pl.multiple_of(i * ROWS, ROWS), ROWS)
                up[r, :] = close(r)
        next_load(l, "pre", "after", "att", "q", "k", "v")
        if l == 0:
            sent[...] = up[length:, :].astype(jnp.bfloat16)
            reply.start()

    reply = remote(sent, came, x_sem.at[0], x_sem.at[1], at.x())
    def start_layer(l):
        down(l)
        expand(l)

    def middle(l):
        open_heads(l)
        fill_up(l)

    before = {0: start_layer, 1: output, 2: middle, 4: fill_out}
    heads = (0, 0, 0, 1, 6, 9, 14, HEADS)
    after = {6: turn}
    later = {7: lambda l: settle(l, 0), 9: lambda l: settle(l, 1), 11: lambda l: settle(l, 2)}
    last = layers - 1
    start_copy = pltpu.make_async_copy(cot_ref, sent, x_sem.at[2])
    start_copy.start()
    for name in ("hidden", "pre", "mixed", "after", "att", "q", "k", "v", "lse"):
        load(last, name).start()
    fetch(last * UNITS + 5).start()
    tiny[...] = jnp.zeros_like(tiny)
    if count(last) < total:
        trio[2, :, count(last) :] = jnp.zeros((width, total - count(last)), jnp.bfloat16)
    at.greet()
    start_copy.wait()
    up[:length, :] = sent[...].astype(jnp.float32)

    @pl.loop(0, reduce.iterations)
    def _(i):
        reduce.step(i)
        phase, layer = lax.rem(i, 2 * UNITS), last - lax.div(i, 2 * UNITS)
        inside = (i < reduce.parts) & (phase >= UNITS)

        def tasks(some):
            for l in range(layers):
                for n, one in some:
                    @pl.when(i == (last - l) * 2 * UNITS + n)
                    def _(one=one, l=l):
                        one(l)

        tasks(before.items())
        first = sum(jnp.where(phase == n, heads[n], 0) for n in range(2, 7))
        final = sum(jnp.where(phase == n, heads[n + 1], 0) for n in range(2, 7))
        for l in range(layers):
            @pl.when((phase >= 2) & (phase < 7) & (layer == l))
            def _(l=l):
                attention(l, first, final)

        tasks(after.items())

        @pl.when(inside & (lax.rem(phase, 2) == 0))
        def _():
            fill_project(lax.div(phase - UNITS, 2))

        @pl.when(inside & (lax.rem(phase, 2) == 1))
        def _():
            project(layer, lax.div(phase - UNITS, 2))

        tasks(later.items())
        reduce.launch(i)
        for n in range(5):
            @pl.when(i == reduce.parts + n)
            def _(n=n):
                reduce.tiny_step(n)
                if n == 2:
                    reply.wait()
                    input_ref[...] = (up[:length, :] + came[...].astype(jnp.float32)).astype(jnp.bfloat16)


def backward_pass(nz, cotangent, full, vec, bias, saved):
    layers = len(saved)
    units = layers * UNITS
    length, width = cotangent.shape
    total = bias.shape[0]
    shard = width // (2 * nz)
    half, wide, low, n = shard // 2, width // 2, nz // 2, nz - 1
    parts = 2 * units
    slots = min(SLOTS, parts)
    flat = [one for group in saved for one in group]
    rows = vec.shape[0]
    dma = pltpu.SemaphoreType.DMA
    small, large = jnp.bfloat16, jnp.float32
    anywhere = pl.BlockSpec(memory_space=pl.ANY)
    inside = pl.BlockSpec(memory_space=pltpu.VMEM)
    natural, turned = (total, width), (width, total)
    return pl.pallas_call(
        functools.partial(backward_kernel, nz, layers, length, total),
        out_shape=(
            jax.ShapeDtypeStruct((units, shard, width), small),
            jax.ShapeDtypeStruct((rows, width), large),
            jax.ShapeDtypeStruct((length, width), small),
        ),
        in_specs=[anywhere, anywhere, inside, inside] + [anywhere] * len(flat),
        out_specs=(anywhere, inside, inside),
        scratch_shapes=[
            pltpu.VMEM(natural, large),
            pltpu.VMEM(natural, large),
            pltpu.VMEM(natural, large),
            pltpu.VMEM(natural, small),
            pltpu.VMEM(natural, small),
            pltpu.VMEM(natural, small),
            pltpu.VMEM(natural, small),
            pltpu.VMEM((3,) + turned, small),
            pltpu.VMEM(turned, small),
            pltpu.VMEM(turned, small),
            pltpu.VMEM((HEADS, 1, total), large),
            pltpu.VMEM((width, width), small),
            pltpu.VMEM((length, width), small),
            pltpu.VMEM((length, width), small),
            dma((layers, 11)),
            dma((1,)),
            dma((3,)),
            pltpu.VMEM((rows, width), large),
            pltpu.VMEM((nz, 2, shard, width), small),
            pltpu.VMEM((slots, nz, half, width), small),
            pltpu.VMEM((parts, low, half, wide), small),
            pltpu.VMEM((parts, low, half, wide), small),
            pltpu.VMEM((parts, 2, half, wide), small),
            pltpu.VMEM((parts, half, wide), small),
            pltpu.VMEM((parts, half, wide), small),
            pltpu.VMEM((3 + n, rows, width), large),
            dma((parts,)), dma((parts,)),
            dma((parts, 2)), dma((parts, 2)),
            dma((parts, 3)), dma((parts, 3)),
            dma((parts,)), dma((parts,)),
            dma((parts,)),
            dma((parts,)), dma((parts,)),
            dma((3 + n,)), dma((3 + n,)),
            pltpu.SemaphoreType.REGULAR,
        ],
        compiler_params=pltpu.CompilerParams(
            collective_id=2, has_side_effects=True, vmem_limit_bytes=63 << 20
        ),
    )(cotangent, full, vec, bias, *flat)


def forward_layer(current, weights, allowed, series_count, local_length, total_length):
    qkv_weight, out_weight, up_weight, down_weight, norm_gains, up_bias, down_bias, query_scale = (
        weights
    )
    token_count, model_width = current.shape
    normed, inverse_one = norm_rows(current, norm_gains[0].astype(jnp.float32))
    normed_low = normed.astype(jnp.bfloat16).reshape(series_count, local_length, model_width)
    projected = jnp.einsum(
        "bld,kdc->bkcl", normed_low, qkv_weight, preferred_element_type=jnp.float32
    ).reshape(series_count, 3 * model_width, local_length)
    query_raw = projected[:, :model_width]
    factor = query_factor(query_scale)
    query_low = (
        query_raw.reshape(series_count, HEADS, HEAD, local_length) * factor[None, None, :, None]
    ).astype(jnp.bfloat16)
    pair_low = projected[:, model_width:].astype(jnp.bfloat16)
    pair_all = lax.all_gather(pair_low, "seq", axis=2, tiled=True)
    key_all = pair_all[:, :model_width].reshape(series_count, HEADS, HEAD, total_length)
    value_all = pair_all[:, model_width:].reshape(series_count, HEADS, HEAD, total_length)
    scores = jnp.einsum("bheq,bhek->bhqk", query_low, key_all, preferred_element_type=jnp.float32)
    scores = jnp.where(allowed[:, None], scores, NEG_FILL)
    top_score = jnp.max(scores, axis=-1, keepdims=True)
    exp_scores = jnp.exp(scores - top_score)
    exp_total = jnp.sum(exp_scores, axis=-1, keepdims=True)
    probs_low = (exp_scores / exp_total).astype(jnp.bfloat16)
    log_total = top_score + jnp.log(exp_total)
    attended = jnp.einsum(
        "bhqk,bhek->bheq", probs_low, value_all, preferred_element_type=jnp.float32
    )
    attended_low = attended.astype(jnp.bfloat16).reshape(series_count, model_width, local_length)
    attn_out = jnp.einsum(
        "bdl,de->ble", attended_low, out_weight, preferred_element_type=jnp.float32
    )
    after_attn = current + attn_out.reshape(token_count, model_width)
    normed_two, inverse_two = norm_rows(after_attn, norm_gains[1].astype(jnp.float32))
    mixed_low = normed_two.astype(jnp.bfloat16)
    hidden_pre = jnp.dot(mixed_low, up_weight, preferred_element_type=jnp.float32) + up_bias.astype(
        jnp.float32
    )
    hidden_low = jax.nn.silu(hidden_pre).astype(jnp.bfloat16)
    result = after_attn + (
        jnp.dot(hidden_low, down_weight, preferred_element_type=jnp.float32)
        + down_bias.astype(jnp.float32)
    )
    stored = (
        current,
        inverse_one,
        normed_low,
        query_raw,
        query_low,
        key_all,
        value_all,
        log_total,
        attended_low,
        after_attn,
        inverse_two,
        mixed_low,
        hidden_pre,
        hidden_low,
    )
    return (result, stored)


def backward_layer(upstream, weights, stored, allowed, series_count, local_length, total_length):
    qkv_weight, out_weight, up_weight, down_weight, norm_gains, up_bias, down_bias, query_scale = (
        weights
    )
    (
        current,
        inverse_one,
        normed_low,
        query_raw,
        query_low,
        key_all,
        value_all,
        log_total,
        attended_low,
        after_attn,
        inverse_two,
        mixed_low,
        hidden_pre,
        hidden_low,
    ) = stored
    token_count, model_width = current.shape
    down_low = upstream.astype(jnp.bfloat16)
    grad_down_bias = jnp.sum(down_low, axis=0, dtype=jnp.float32)
    grad_down = jnp.einsum("tf,td->fd", hidden_low, down_low, preferred_element_type=jnp.float32)
    hidden_grad = jnp.einsum("td,fd->tf", down_low, down_weight, preferred_element_type=jnp.float32)
    sigmoid_pre = jax.nn.sigmoid(hidden_pre)
    pre_low = (hidden_grad * sigmoid_pre * (1.0 + hidden_pre * (1.0 - sigmoid_pre))).astype(
        jnp.bfloat16
    )
    grad_up_bias = jnp.sum(pre_low, axis=0, dtype=jnp.float32)
    grad_up = jnp.einsum("td,tf->df", mixed_low, pre_low, preferred_element_type=jnp.float32)
    mixed_grad = jnp.einsum("tf,df->td", pre_low, up_weight, preferred_element_type=jnp.float32)
    norm_grad_two, gain_grad_two = norm_back(
        after_attn, inverse_two, norm_gains[1].astype(jnp.float32), mixed_grad
    )
    attn_grad = upstream + norm_grad_two
    branch_low = attn_grad.astype(jnp.bfloat16).reshape(series_count, local_length, model_width)
    grad_out = jnp.einsum(
        "bdl,ble->de", attended_low, branch_low, preferred_element_type=jnp.float32
    )
    output_low = (
        jnp.einsum("ble,de->bdl", branch_low, out_weight, preferred_element_type=jnp.float32)
        .astype(jnp.bfloat16)
        .reshape(series_count, HEADS, HEAD, local_length)
    )
    scores = jnp.einsum("bheq,bhek->bhqk", query_low, key_all, preferred_element_type=jnp.float32)
    scores = jnp.where(allowed[:, None], scores, NEG_FILL)
    attn_probs = jnp.exp(scores - log_total)
    prob_grad = jnp.einsum(
        "bheq,bhek->bhqk", output_low, value_all, preferred_element_type=jnp.float32
    )
    row_inner = jnp.sum(attn_probs * prob_grad, axis=-1, keepdims=True)
    score_low = (attn_probs * (prob_grad - row_inner)).astype(jnp.bfloat16)
    value_grad = jnp.einsum(
        "bhqk,bheq->bhek",
        attn_probs.astype(jnp.bfloat16),
        output_low,
        preferred_element_type=jnp.float32,
    )
    key_grad = jnp.einsum(
        "bhqk,bheq->bhek", score_low, query_low, preferred_element_type=jnp.float32
    )
    query_grad = jnp.einsum(
        "bhqk,bhek->bheq", score_low, key_all, preferred_element_type=jnp.float32
    )
    pair_grad = jnp.concatenate(
        [
            key_grad.reshape(series_count, model_width, total_length),
            value_grad.reshape(series_count, model_width, total_length),
        ],
        axis=1,
    )
    pair_local = lax.psum_scatter(pair_grad, "seq", scatter_dimension=2, tiled=True)
    key_local, value_local = pair_local[:, :model_width], pair_local[:, model_width:]
    factor = query_factor(query_scale)
    factor_grad = jnp.sum(
        query_grad * query_raw.reshape(series_count, HEADS, HEAD, local_length), axis=(0, 1, 3)
    )
    grad_scale = (
        factor_grad * jax.nn.sigmoid(query_scale.astype(jnp.float32)) * (SOFT_ONE / math.sqrt(HEAD))
    )
    raw_low = (
        (query_grad * factor[None, None, :, None])
        .astype(jnp.bfloat16)
        .reshape(series_count, model_width, local_length)
    )
    projected_grad = jnp.concatenate(
        [raw_low, key_local.astype(jnp.bfloat16), value_local.astype(jnp.bfloat16)], axis=1
    )
    grad_qkv = jnp.einsum(
        "bld,bcl->dc", normed_low, projected_grad, preferred_element_type=jnp.float32
    )
    normed_grad = jnp.einsum(
        "bkcl,kdc->bld",
        projected_grad.reshape(series_count, 3, model_width, local_length),
        qkv_weight,
        preferred_element_type=jnp.float32,
    ).reshape(token_count, model_width)
    norm_grad_one, gain_grad_one = norm_back(
        current, inverse_one, norm_gains[0].astype(jnp.float32), normed_grad
    )
    result = attn_grad + norm_grad_one
    layer_grads = (
        grad_qkv,
        grad_out,
        grad_up,
        grad_down,
        jnp.stack([gain_grad_one, gain_grad_two]),
        grad_up_bias,
        grad_down_bias,
        grad_scale,
    )
    return (result, layer_grads)


def pack_small(norm_gains, up_bias, down_bias, query_scale):
    layers, _, shard = norm_gains.shape
    scale = jnp.pad(query_scale, ((0, 0), (0, shard - query_scale.shape[1])))
    rows = jnp.concatenate([norm_gains.reshape(2 * layers, shard), up_bias, down_bias, scale])
    return jnp.pad(rows, ((0, -rows.shape[0] % 16), (0, -shard % 128)))


def unpack_small(tiny, layers, shard, scale_shard):
    count = tiny.shape[0]
    vectors = tiny[:, : 4 * layers, :shard].transpose(1, 0, 2).reshape(4 * layers, count * shard)
    scale = tiny[:, 4 * layers : 5 * layers, :scale_shard].transpose(1, 0, 2).reshape(layers, count * scale_shard)
    gains = vectors[: 2 * layers].reshape(layers, 2, count * shard)
    return gains, vectors[2 * layers : 3 * layers], vectors[3 * layers :], scale


def pack_tiny(layer_grads, count):
    gains = jnp.concatenate([g[4] for g in layer_grads])
    vectors = jnp.concatenate(
        [gains, jnp.stack([g[5] for g in layer_grads]), jnp.stack([g[6] for g in layer_grads])]
    )
    scale = jnp.stack([g[7] for g in layer_grads])
    shard, part = vectors.shape[1] // count, scale.shape[1] // count
    vectors = vectors.reshape(-1, count, shard)
    scale = jnp.pad(scale.reshape(-1, count, part), ((0, 0), (0, 0), (0, shard - part)))
    rows = jnp.concatenate([vectors, scale]).transpose(1, 0, 2)
    return jnp.pad(rows, ((0, 0), (0, -rows.shape[1] % 16), (0, -shard % 128)))


def unpack_tiny(tiny, layers, shard, part):
    gains = tiny[: 2 * layers, :shard].reshape(layers, 2, shard)
    up, down = tiny[2 * layers : 3 * layers, :shard], tiny[3 * layers : 4 * layers, :shard]
    return gains, up, down, tiny[4 * layers : 5 * layers, :part]


def gather_plain(qkv_weight, out_weight, up_weight, down_weight, small):
    layers, shard, width = out_weight.shape
    qkv = qkv_weight.reshape(layers, shard, 3, width).transpose(0, 2, 1, 3)
    square = jnp.stack([out_weight, up_weight, down_weight], axis=1)
    units = jnp.concatenate([qkv, square], axis=1).reshape(layers * UNITS, shard, width)
    full = lax.all_gather(units, "fsdp", axis=1, tiled=True)
    return full, lax.all_gather(small, "fsdp", axis=0)


def reduce_plain(layer_grads, tiny):
    units = []
    for grads in layer_grads:
        width = grads[0].shape[1]
        units += list(grads[:3]) + [grads[3][:, k * width : (k + 1) * width] for k in range(3)]
    shares = lax.psum_scatter(jnp.stack(units), "fsdp", scatter_dimension=1, tiled=True)
    small = lax.psum_scatter(tiny, "fsdp", scatter_dimension=0, tiled=True)[0]
    return lax.psum(shares, ("replica", "seq")), lax.psum(small, ("replica", "seq"))


def plain(
    series_in,
    cotangent,
    qkv_weight,
    out_weight,
    up_weight,
    down_weight,
    norm_gains,
    up_bias,
    down_bias,
    query_scale,
    pad_length,
    span_starts,
    span_count,
):
    series_count, local_length, model_width = series_in.shape
    seq_count = lax.axis_size("seq")
    group = lax.axis_size("fsdp")
    total_length = local_length * seq_count
    offset = lax.axis_index("seq") * local_length
    allowed = visible(pad_length, span_starts, span_count, offset, local_length, total_length)
    layer_count, shard = qkv_weight.shape[:2]
    scale_shard = query_scale.shape[1]
    small = pack_small(norm_gains, up_bias, down_bias, query_scale)
    full, tiny = gather_plain(qkv_weight, out_weight, up_weight, down_weight, small)
    gains, up_full, down_full, scale_full = unpack_small(tiny, layer_count, shard, scale_shard)
    weights = [
        (
            full[UNITS * l : UNITS * l + 3],
            full[UNITS * l + 3],
            full[UNITS * l + 4],
            full[UNITS * l + 5],
            gains[l],
            up_full[l],
            down_full[l],
            scale_full[l],
        )
        for l in range(layer_count)
    ]
    current = series_in.reshape(series_count * local_length, model_width).astype(jnp.float32)
    stored_list = []
    for l in range(layer_count):
        current, stored = forward_layer(
            current, weights[l], allowed, series_count, local_length, total_length
        )
        stored_list.append(stored)
    series_out = current.reshape(series_count, local_length, model_width).astype(jnp.bfloat16)
    upstream = cotangent.reshape(series_count * local_length, model_width).astype(jnp.float32)
    order = list(reversed(range(layer_count)))
    grads_list = {}
    for l in order:
        upstream, grads_list[l] = backward_layer(
            upstream, weights[l], stored_list[l], allowed, series_count, local_length, total_length
        )
    tiny_grads = pack_tiny([grads_list[l] for l in range(layer_count)], group)
    big = [
        tuple(grads_list[l][k].astype(jnp.bfloat16) for k in (3, 2, 1, 0)) for l in order
    ]
    shares, tiny_sum = reduce_plain(big, tiny_grads)
    shares = shares.reshape(layer_count, UNITS, shard, model_width)[::-1]
    grad_gains, grad_up_bias, grad_down_bias, grad_scale = unpack_tiny(
        tiny_sum, layer_count, shard, scale_shard
    )
    grad_qkv = shares[:, 3:].transpose(0, 2, 1, 3).reshape(layer_count, shard, 3 * model_width)
    input_grad = upstream.reshape(series_count, local_length, model_width).astype(jnp.bfloat16)
    return (
        series_out,
        input_grad,
        grad_qkv.astype(jnp.float32),
        shares[:, 2].astype(jnp.float32),
        shares[:, 1].astype(jnp.float32),
        shares[:, 0].astype(jnp.float32),
        grad_gains,
        grad_up_bias,
        grad_down_bias,
        grad_scale,
    )


def finish(shares, tiny, layers, shard, width, query_scale):
    shares = shares.reshape(layers, UNITS, shard, width)[::-1]
    low = jnp.float32
    place = lax.axis_index("fsdp")
    part = query_scale.shape[1]
    vectors = lax.dynamic_slice_in_dim(tiny[: 4 * layers], place * shard, shard, axis=1)
    scale = lax.dynamic_slice_in_dim(tiny[4 * layers : 5 * layers], place * part, part, axis=1)
    raw = query_scale.astype(jnp.float32)
    scale = scale * (jax.nn.sigmoid(raw) * (SOFT_ONE / math.sqrt(HEAD))) / query_factor(query_scale)
    qkv = jnp.concatenate([shares[:, 5], shares[:, 3], shares[:, 4]], axis=2)
    return (
        qkv.astype(low),
        shares[:, 2].astype(low),
        shares[:, 1].astype(low),
        shares[:, 0].astype(low),
        vectors[: 2 * layers].reshape(layers, 2, shard),
        vectors[2 * layers : 3 * layers],
        vectors[3 * layers :],
        scale,
    )


def fused(
    series_in,
    cotangent,
    qkv_weight,
    out_weight,
    up_weight,
    down_weight,
    norm_gains,
    up_bias,
    down_bias,
    query_scale,
    pad_length,
    span_starts,
    span_count,
):
    layers, shard, width = out_weight.shape
    nz = lax.axis_size("fsdp") // 2
    full, vec, series_out, bias, saved = forward_pass(
        nz,
        series_in[0],
        (qkv_weight, out_weight, up_weight, down_weight),
        (norm_gains, up_bias, down_bias, query_scale),
        (pad_length, span_starts, span_count),
    )
    shares, tiny, input_grad = backward_pass(nz, cotangent[0], full, vec, bias, saved)
    rest = finish(shares, tiny, layers, shard, width, query_scale)
    return (series_out[None], input_grad[None]) + rest


def shards(*args):
    series_in, out_weight = args[0], args[3]
    group = lax.axis_size("fsdp")
    width = series_in.shape[2]
    block = lax.axis_size("replica") == 2 and lax.axis_size("seq") == 2 and group == 8
    block = block and series_in.shape[0] == 1 and width == out_weight.shape[2] == HEADS * HEAD
    block = block and (width // group) % 32 == 0 and width % 256 == 0
    return fused(*args) if block else plain(*args)


def solution(mesh):
    return jax.shard_map(
        shards,
        mesh=mesh,
        in_specs=(
            P(("replica", "fsdp"), "seq", None),
            P(("replica", "fsdp"), "seq", None),
            P(None, "fsdp", None),
            P(None, "fsdp", None),
            P(None, "fsdp", None),
            P(None, "fsdp", None),
            P(None, None, "fsdp"),
            P(None, "fsdp"),
            P(None, "fsdp"),
            P(None, "fsdp"),
            P(("replica", "fsdp")),
            P(("replica", "fsdp"), None),
            P(("replica", "fsdp")),
        ),
        out_specs=(
            P(("replica", "fsdp"), "seq", None),
            P(("replica", "fsdp"), "seq", None),
            P(None, "fsdp", None),
            P(None, "fsdp", None),
            P(None, "fsdp", None),
            P(None, "fsdp", None),
            P(None, None, "fsdp"),
            P(None, "fsdp"),
            P(None, "fsdp"),
            P(None, "fsdp"),
        ),
        check_vma=False,
    )
```

profile of v0, /device:TPU:0, one launch (start us, length us, event | category | flops | bytes accessed | tf_op | source)
XLA Modules:
  0.0 392.6 jit_solution(6345422667866363037)
XLA Ops:
  1.9 162.1 %shard_map.204 = (bf16[12,1280,1280]{2,1,0:T(8,128)(2,1)}, f32[16,1280]{1,0:T(8,128)}, bf16[256,1280]{1,0:T(8,128)(2,1)}, f32[512,512]{1,0:T(8,128)}, bf16[512,1...) custom-call(bf16[256,1280]{1,0:T(8,128)(2,1)} %bitcast.34, ...), custom_call_target="tpu_custom_call" | custom-call | tf_op jit(solution)/shard_map/pallas_call | solution.py:648
  164.0 216.1 %shard_map.205 = (bf16[12,160,1280]{2,1,0:T(8,128)(2,1)}, f32[16,1280]{1,0:T(8,128)}, bf16[256,1280]{1,0:T(8,128)(2,1)}) custom-call(bf16[256,1280]{1,0:T(8,128)(2,1)} %bitcast.33, bf16[12,1280,1280]{2,1,0:T(8,128)(2,1)} %get-tuple-element.40.refs_1_, f32[16,1280]{1,0:T(8,128)} %get-tuple-element.41.refs_2_, f32[512,512]{1,0:T(8,128)} %get-tuple-element.42.refs_3_, ...), custom_call_target="tpu_custom_call" | custom-call | tf_op jit(solution)/shard_map/pallas_call | solution.py:1175
  380.2 2.7 slice_bitcast_fusion
  382.9 1.3 bitcast_convert_fusion.2
  384.2 0.1 reverse_bitcast_fusion.1
  384.3 2.6 maximum_convert_fusion
  386.9 0.0 copy-start.2
  386.9 0.0 copy-start.3
  386.9 0.0 copy-start
  386.9 2.0 bitcast_convert_fusion
  388.9 0.0 copy-start.1
  388.9 0.0 copy-done.2
  388.9 0.1 constant_dynamic-slice_fusion
  389.0 0.6 reshape.33
  389.6 0.7 fusion.11
  390.3 0.0 copy-done.3
  390.3 0.6 fusion.5
  390.9 0.0 copy-done
  390.9 0.8 copy.39
  391.8 0.0 copy-done.1
  391.8 0.8 copy.40
  (2 shorter events, 0.0 us)
Async XLA Ops:
  386.9 2.0 copy-start.2
  386.9 3.4 copy-start.3
  386.9 4.0 %copy-start = (bf16[256,1280]{1,0:T(8,128)(2,1)S(1)}, bf16[256,1280]{1,0:T(8,128)(2,1)}, u32[]{:S(2)}) copy-start(bf16[256,1280]{1,0:T(8,128)(2,1)} %get-tuple-element.39) | copy-start | bytes 1966084
  388.9 2.9 copy-start.1
where the time goes:
time: 393 us
  Pallas kernels  378 us (96%)
  other arithmetic  6.54 us (2%)
  local copies, waits for them, and re-layouts  5.86 us (1%)
    pallas_call x1, Pallas kernels, backward_pass(): pl.pallas_call(functools.partial(backward_kernel, nz, layers, length, tot...  216 us
    pallas_call x1, Pallas kernels, forward_pass(): pl.pallas_call(functools.partial(forward_kernel, nz, layers, part), out_s...  162 us

commit v1 on v0

--- a/solution.py
+++ b/solution.py
@@ -58,6 +58,9 @@
 MESH = pl.DeviceIdType.MESH
 UNITS = 6
 LAG = 1
+PASS = 1
+TURN = 1
+TOP = 40
 
 
 class Place:
@@ -110,7 +113,7 @@
         self.half, self.wide = self.shard // 2, self.width // 2
         self.units = layers * UNITS
         self.hops = nz - 1
-        self.iterations = self.units + LAG * (self.hops + 2)
+        self.iterations = self.units + LAG * self.hops + PASS + TURN
 
     def source(self, way, k):
         return self.at.z - way * k
@@ -136,10 +139,11 @@
         return self.full_ref.at[u, pl.ds(row, self.half), pl.ds(col, self.wide)]
 
     def quarter(self, u, z, c, r, s, part):
-        step = self.half // 2
-        row = pl.multiple_of((2 * z + c) * self.shard + r * self.half + part * step, 8)
+        top = self.half * TOP // 80 // 8 * 8
+        row = pl.multiple_of((2 * z + c) * self.shard + r * self.half + part * top, 8)
         col = pl.multiple_of(s * self.wide, 128)
-        return self.full_ref.at[u, pl.ds(row, step), pl.ds(col, self.wide)]
+        size = self.half - top if part else top
+        return self.full_ref.at[u, pl.ds(row, size), pl.ds(col, self.wide)]
 
     def own(self, u, c):
         row = pl.multiple_of((2 * self.at.z + c) * self.shard, 8)
@@ -300,9 +304,9 @@
         for k in range(1, self.hops + 1):
             stage(LAG * k, lambda u, k=k: self.hop(u, k))
         for k in range(1, self.hops + 1):
-            stage(LAG * (k + 1), lambda u, k=k: self.forward(u, k))
+            stage(LAG * k + PASS, lambda u, k=k: self.forward(u, k))
         for k in range(2, self.hops + 1):
-            stage(LAG * (k + 2), lambda u, k=k: self.diagonal(u, k))
+            stage(LAG * k + PASS + TURN, lambda u, k=k: self.diagonal(u, k))
 
     def ready(self, u):
         self.keep(u).wait()
@@ -370,6 +374,7 @@
 ROWS = 128
 TALL = 256
 BEGIN = 3
+SOON = 5
 
 
 def each_tile(count, body, rows=ROWS):
@@ -574,8 +579,9 @@
         computing.append([lambda l=l: contract(l)])
     for u in range(units):
         add(u + lag, lambda u=u: pull(u))
+        late = u >= units - SOON
         for one in computing[u]:
-            add(min(u + lag + 1, gather.iterations - 1), one)
+            add(u + lag + (0 if late else 1), one)
 
     own_copy.start()
     small_ref[...] = jnp.zeros_like(small_ref)
@@ -1086,7 +1092,6 @@
         next_load(l, "pre", "after", "att", "q", "k", "v")
         if l == 0:
             sent[...] = up[length:, :].astype(jnp.bfloat16)
-            reply.start()
 
     reply = remote(sent, came, x_sem.at[0], x_sem.at[1], at.x())
     def start_layer(l):
@@ -1147,13 +1152,18 @@
 
         tasks(later.items())
         reduce.launch(i)
+
+        @pl.when(i == reduce.parts)
+        def _():
+            reply.start()
+
         for n in range(5):
-            @pl.when(i == reduce.parts + n)
+            @pl.when(i == reduce.parts + 1 + 2 * n)
             def _(n=n):
                 reduce.tiny_step(n)
-                if n == 2:
-                    reply.wait()
-                    input_ref[...] = (up[:length, :] + came[...].astype(jnp.float32)).astype(jnp.bfloat16)
+
+    reply.wait()
+    input_ref[...] = (up[:length, :] + came[...].astype(jnp.float32)).astype(jnp.bfloat16)
 
 
 def backward_pass(nz, cotangent, full, vec, bias, saved):

time: 393 us -> 381 us (0.969)
  Pallas kernels: 378 us -> 366 us
    pallas_call x1, Pallas kernels: 216 us -> 204 us  [backward_pass(): pl.pallas_call(functools.partial(backward_kernel, nz, layers, length, tot...]
where the time goes in v1:
time: 381 us; the launch traced here: 380 us
  Pallas kernels  366 us (96%)
  other arithmetic  6.54 us (2%)
  local copies, waits for them, and re-layouts  5.86 us (2%)
    pallas_call x1, Pallas kernels, backward_pass(): pl.pallas_call(functools.partial(backward_kernel, nz, layers, length, tot...  204 us
    pallas_call x1, Pallas kernels, forward_pass(): pl.pallas_call(functools.partial(forward_kernel, nz, layers, part), out_s...  162 us

profile of v1, /device:TPU:0, one launch (start us, length us, event | category | flops | bytes accessed | tf_op | source)
XLA Modules:
  0.0 380.4 jit_solution(8771440176119733942)
XLA Ops:
  1.9 162.2 %shard_map.204 = (bf16[12,1280,1280]{2,1,0:T(8,128)(2,1)}, f32[16,1280]{1,0:T(8,128)}, bf16[256,1280]{1,0:T(8,128)(2,1)}, f32[512,512]{1,0:T(8,128)}, bf16[512,1...) custom-call(bf16[256,1280]{1,0:T(8,128)(2,1)} %bitcast.34, ...), custom_call_target="tpu_custom_call" | custom-call | tf_op jit(solution)/shard_map/pallas_call | solution.py:654
  164.1 203.8 %shard_map.205 = (bf16[12,160,1280]{2,1,0:T(8,128)(2,1)}, f32[16,1280]{1,0:T(8,128)}, bf16[256,1280]{1,0:T(8,128)(2,1)}) custom-call(bf16[256,1280]{1,0:T(8,128)(2,1)} %bitcast.33, bf16[12,1280,1280]{2,1,0:T(8,128)(2,1)} %get-tuple-element.40.refs_1_, f32[16,1280]{1,0:T(8,128)} %get-tuple-element.41.refs_2_, f32[512,512]{1,0:T(8,128)} %get-tuple-element.42.refs_3_, ...), custom_call_target="tpu_custom_call" | custom-call | tf_op jit(solution)/shard_map/pallas_call | solution.py:1185
  367.9 2.7 slice_bitcast_fusion
  370.7 1.3 bitcast_convert_fusion.2
  372.0 0.1 reverse_bitcast_fusion.1
  372.1 2.6 maximum_convert_fusion
  374.7 0.0 copy-start.2
  374.7 0.0 copy-start.3
  374.7 0.0 copy-start
  374.7 2.0 bitcast_convert_fusion
  376.7 0.0 copy-start.1
  376.7 0.0 copy-done.2
  376.7 0.1 constant_dynamic-slice_fusion
  376.8 0.6 reshape.33
  377.4 0.7 fusion.11
  378.0 0.0 copy-done.3
  378.0 0.6 fusion.5
  378.7 0.0 copy-done
  378.7 0.8 copy.39
  379.5 0.0 copy-done.1
  379.5 0.8 copy.40
  (2 shorter events, 0.0 us)
Async XLA Ops:
  374.7 2.0 copy-start.2
  374.7 3.4 copy-start.3
  374.7 4.0 %copy-start = (bf16[256,1280]{1,0:T(8,128)(2,1)S(1)}, bf16[256,1280]{1,0:T(8,128)(2,1)}, u32[]{:S(2)}) copy-start(bf16[256,1280]{1,0:T(8,128)(2,1)} %get-tuple-element.39) | copy-start | bytes 1966084
  376.7 2.9 copy-start.1

commit v2 on v1

--- a/solution.py
+++ b/solution.py
@@ -88,12 +88,16 @@
     def source(self, d):
         return lax.rem(self.z - d + self.nz, self.nz)
 
-    def greet(self):
+    def peers(self):
+        return [self.x(), self.y(), self.core()] + [self.to(d) for d in range(1, self.nz)]
+
+    def hail(self):
         barrier = pltpu.get_barrier_semaphore()
-        peers = [self.x(), self.y(), self.core()] + [self.to(d) for d in range(1, self.nz)]
-        for peer in peers:
+        for peer in self.peers():
             pl.semaphore_signal(barrier, inc=1, device_id=peer, device_id_type=MESH)
-        pl.semaphore_wait(barrier, len(peers))
+
+    def hear(self):
+        pl.semaphore_wait(pltpu.get_barrier_semaphore(), len(self.peers()))
 
 
 def remote(src, dst, send, recv, device):
@@ -227,7 +231,7 @@
         for layer in range(self.layers):
             for k in range(UNITS):
                 self.local(layer, k).start()
-        self.at.greet()
+        self.at.hear()
         for d in range(1, self.nz):
             self.tiny(d).start()
         self.tiny_core(0).start()
@@ -459,6 +463,13 @@
     def fetch(u):
         return pltpu.make_async_copy(full_ref.at[u], weights.at[u % 2], load_sem.at[u % 2])
 
+    units = layers * UNITS
+
+    def half_fetch(n):
+        c = pl.ds(n * gather.wide, gather.wide)
+        home = weights.at[(units - 1) % 2, :, c]
+        return pltpu.make_async_copy(full_ref.at[units - 1, :, c], home, load_sem.at[2 + n])
+
     def arrived(u):
         fetch(u).wait()
         return weights.at[u % 2]
@@ -524,23 +535,32 @@
         save(l, 9).start()
         save(l, 10).start()
 
+    def close_out(l):
+        b = held[l]
+        bias = vector(3 * layers + l)
+        for n in range(2):
+            half_fetch(n).wait()
+            c = slice(n * gather.wide, (n + 1) * gather.wide)
+
+            def body(r, c=c):
+                values = b["after"][r, c] + (dot_nn(b["hidden"][r, :], weights[(units - 1) % 2, :, c]) + bias[:, c])
+                last[r, c] = values.astype(jnp.bfloat16)
+            each_tile(b["after"].shape[0], body)
+        pltpu.make_async_copy(last, series_out, swap_sem.at[3]).start()
+
     def contract(l):
+        if l + 1 == layers:
+            return close_out(l)
         b = held[l]
         weight = arrived(l * UNITS + 5)
         bias = vector(3 * layers + l)
 
         def body(r):
             values = b["after"][r, :] + (dot_nn(b["hidden"][r, :], weight[...]) + bias)
-            if l + 1 < layers:
-                held[l + 1]["current"][r, :] = values
-            else:
-                last[r, :] = values.astype(jnp.bfloat16)
+            held[l + 1]["current"][r, :] = values
         each_tile(b["after"].shape[0], body)
-        if l + 1 < layers:
-            save(l + 1, 0).start()
-            normalize(l + 1)
-        else:
-            pltpu.make_async_copy(last, series_out, swap_sem.at[3]).start()
+        save(l + 1, 0).start()
+        normalize(l + 1)
 
     tasks = {}
 
@@ -565,7 +585,11 @@
 
     def pull(u):
         gather.ready(u)
-        fetch(u).start()
+        if u < units - 1:
+            fetch(u).start()
+            return
+        for n in range(2):
+            half_fetch(n).start()
 
     add(1, early)
     add(BEGIN, begin)
@@ -583,6 +607,7 @@
         for one in computing[u]:
             add(u + lag + (0 if late else 1), one)
 
+    at.hail()
     own_copy.start()
     small_ref[...] = jnp.zeros_like(small_ref)
     shard = gather.shard
@@ -672,7 +697,7 @@
             pltpu.VMEM(small, wide),
             pltpu.VMEM((total, total), wide),
             dma((6,)),
-            dma((2,)),
+            dma((4,)),
             dma((layers, 11)),
         ]
         + gather_scratch(nz, layers, shard, width),
@@ -1108,6 +1133,7 @@
     later = {7: lambda l: settle(l, 0), 9: lambda l: settle(l, 1), 11: lambda l: settle(l, 2)}
     last = layers - 1
     start_copy = pltpu.make_async_copy(cot_ref, sent, x_sem.at[2])
+    at.hail()
     start_copy.start()
     for name in ("hidden", "pre", "mixed", "after", "att", "q", "k", "v", "lse"):
         load(last, name).start()
@@ -1115,9 +1141,10 @@
     tiny[...] = jnp.zeros_like(tiny)
     if count(last) < total:
         trio[2, :, count(last) :] = jnp.zeros((width, total - count(last)), jnp.bfloat16)
-    at.greet()
     start_copy.wait()
     up[:length, :] = sent[...].astype(jnp.float32)
+    start_layer(last)
+    at.hear()
 
     @pl.loop(0, reduce.iterations)
     def _(i):
@@ -1128,6 +1155,9 @@
         def tasks(some):
             for l in range(layers):
                 for n, one in some:
+                    if l == last and n == 0:
+                        continue
+
                     @pl.when(i == (last - l) * 2 * UNITS + n)
                     def _(one=one, l=l):
                         one(l)

time: 381 us -> 381 us (level)
  no operation moved by 1% of the time
where the time goes in v2:
time: 381 us; the launch traced here: 380 us
  Pallas kernels  366 us (96%)
  other arithmetic  6.54 us (2%)
  local copies, waits for them, and re-layouts  5.86 us (2%)
    pallas_call x1, Pallas kernels, backward_pass(): pl.pallas_call(functools.partial(backward_kernel, nz, layers, length, tot...  204 us
    pallas_call x1, Pallas kernels, forward_pass(): pl.pallas_call(functools.partial(forward_kernel, nz, layers, part), out_s...  162 us

profile of v2, /device:TPU:0, one launch (start us, length us, event | category | flops | bytes accessed | tf_op | source)
XLA Modules:
  0.0 380.3 jit_solution(4580834898192744795)
XLA Ops:
  1.9 162.3 %shard_map.204 = (bf16[12,1280,1280]{2,1,0:T(8,128)(2,1)}, f32[16,1280]{1,0:T(8,128)}, bf16[256,1280]{1,0:T(8,128)(2,1)}, f32[512,512]{1,0:T(8,128)}, bf16[512,1...) custom-call(bf16[256,1280]{1,0:T(8,128)(2,1)} %bitcast.34, ...), custom_call_target="tpu_custom_call" | custom-call | tf_op jit(solution)/shard_map/pallas_call | solution.py:679
  164.2 203.6 %shard_map.205 = (bf16[12,160,1280]{2,1,0:T(8,128)(2,1)}, f32[16,1280]{1,0:T(8,128)}, bf16[256,1280]{1,0:T(8,128)(2,1)}) custom-call(bf16[256,1280]{1,0:T(8,128)(2,1)} %bitcast.33, bf16[12,1280,1280]{2,1,0:T(8,128)(2,1)} %get-tuple-element.40.refs_1_, f32[16,1280]{1,0:T(8,128)} %get-tuple-element.41.refs_2_, f32[512,512]{1,0:T(8,128)} %get-tuple-element.42.refs_3_, ...), custom_call_target="tpu_custom_call" | custom-call | tf_op jit(solution)/shard_map/pallas_call | solution.py:1215
  367.9 2.7 slice_bitcast_fusion
  370.6 1.3 bitcast_convert_fusion.2
  371.9 0.1 reverse_bitcast_fusion.1
  372.0 2.6 maximum_convert_fusion
  374.6 0.0 copy-start.2
  374.6 0.0 copy-start.3
  374.6 0.0 copy-start
  374.6 2.0 bitcast_convert_fusion
  376.6 0.0 copy-start.1
  376.6 0.0 copy-done.2
  376.6 0.1 constant_dynamic-slice_fusion
  376.7 0.6 reshape.33
  377.3 0.7 fusion.11
  378.0 0.0 copy-done.3
  378.0 0.6 fusion.5
  378.6 0.0 copy-done
  378.6 0.8 copy.39
  379.4 0.0 copy-done.1
  379.4 0.8 copy.40
  (2 shorter events, 0.0 us)
Async XLA Ops:
  374.6 2.0 copy-start.2
  374.6 3.4 copy-start.3
  374.6 4.0 %copy-start = (bf16[256,1280]{1,0:T(8,128)(2,1)S(1)}, bf16[256,1280]{1,0:T(8,128)(2,1)}, u32[]{:S(2)}) copy-start(bf16[256,1280]{1,0:T(8,128)(2,1)} %get-tuple-element.39) | copy-start | bytes 1966084
  376.6 2.9 copy-start.1
